TPU v7x, 32 devices: a whole 2x2x4 slice. The times are simulated.
32 devices in a mesh: dp: 2 (over x), expert: 16 (over z, y, core).
Axes of the slice: x: 2, y: 2, z: 4, core: 2. Of those that a mesh axis runs over, the one named last changes fastest.
Arguments:
- tokens: bfloat16 [512, 4096], P('expert'), may hold values from -6 to 6
- expert_ids: int32 [512, 8], P('expert'), may hold values from 0 to 15, all different within a row; in each aligned block of 32 rows (0 to 31, 32 to 63, ...) at most 24 rows name the same one
- gate_ints: int32 [512, 8], P('expert'), may hold values from 1 to 1024
- w_gate: bfloat16 [16, 4096, 1536], P('expert', None, 'dp'), may hold values from -0.09375 to 0.09375
- w_up: bfloat16 [16, 4096, 1536], P('expert', None, 'dp'), may hold values from -0.09375 to 0.09375
- w_down: bfloat16 [16, 1536, 4096], P('expert', 'dp'), may hold values from -0.15625 to 0.15625
Outputs:
- mixed: bfloat16 [512, 4096], P('expert')
Inputs may be any that keep to these rules, and one draw needn't show every extreme that they name: `expert_ids`: within the rows of one device each expert is named at most 24 times, and each row names 8 different experts.
All inputs are finite; a program needn't handle non-finite values.
Results may differ from a plain program's by a relative error of at most 0.017.
Values may be sent and summed in bfloat16 or wider, within the bound.
A program may use at most 64 MiB of HBM per device.

v0:
```python
import jax
import jax.numpy as jnp
from jax import lax
from jax.sharding import PartitionSpec as P


def on_device(tokens, expert_ids, gate_ints, w_gate, w_up, w_down):
    tok_rows = tokens.shape[0]
    top_count = expert_ids.shape[1]
    feature = tokens.shape[1]
    groups = lax.axis_size("expert")
    capacity = min(tok_rows, max(2, 3 * tok_rows * top_count // (2 * groups)))
    pairs = tok_rows * top_count
    flat_ids = expert_ids.reshape(pairs)
    onehot = (flat_ids[:, None] == jnp.arange(groups, dtype=jnp.int32)[None, :]).astype(jnp.int32)
    before = jnp.cumsum(onehot, axis=0) - onehot
    slot = jnp.sum(before * onehot, axis=1)
    target = flat_ids * capacity + slot
    select = (jnp.arange(groups * capacity, dtype=jnp.int32)[:, None] == target[None, :]).astype(
        jnp.bfloat16
    )
    owner = (
        (jnp.arange(pairs, dtype=jnp.int32) // top_count)[:, None]
        == jnp.arange(tok_rows, dtype=jnp.int32)[None, :]
    ).astype(jnp.bfloat16)
    placing = jnp.dot(select, owner, preferred_element_type=jnp.float32).astype(jnp.bfloat16)
    outgoing = jnp.dot(placing, tokens, preferred_element_type=jnp.float32).astype(jnp.bfloat16)
    arrived = lax.all_to_all(
        outgoing.reshape(groups, capacity, feature),
        "expert",
        split_axis=0,
        concat_axis=0,
        tiled=True,
    )
    rows = arrived.reshape(groups * capacity, feature)
    gate = jnp.dot(rows, w_gate[0], preferred_element_type=jnp.float32)
    up = jnp.dot(rows, w_up[0], preferred_element_type=jnp.float32)
    hidden = (jax.nn.silu(gate) * up).astype(jnp.bfloat16)
    partial_value = jnp.dot(hidden, w_down[0], preferred_element_type=jnp.float32).astype(
        jnp.bfloat16
    )
    back = lax.all_to_all(
        partial_value.reshape(groups, capacity, feature),
        "expert",
        split_axis=0,
        concat_axis=0,
        tiled=True,
    )
    back_rows = back.reshape(groups * capacity, feature)
    weights = (gate_ints.astype(jnp.float32) / 1024.0)[:, :, None]
    picked = (
        jnp.take(back_rows, target, axis=0)
        .reshape(tok_rows, top_count, feature)
        .astype(jnp.float32)
    )
    local_mix = jnp.sum(weights * picked, axis=1)
    mixed = lax.psum(local_mix.astype(jnp.bfloat16), "dp")
    return mixed


def solution(mesh):
    return jax.shard_map(
        on_device,
        mesh=mesh,
        in_specs=(
            P("expert", None),
            P("expert", None),
            P("expert", None),
            P("expert", None, "dp"),
            P("expert", None, "dp"),
            P("expert", "dp", None),
        ),
        out_specs=P("expert", None),
        check_vma=False,
    )
```

profile of v0, /device:TPU:0, one launch (start us, length us, event | category | flops | bytes accessed | tf_op | source)
XLA Modules:
  0.0 219.8 jit_solution(6239488634698124795)
XLA Ops:
  6.5 0.0 copy-start
  6.5 0.8 copy.10
  7.3 0.1 eq.52
  7.4 0.1 reshape.96
  7.5 0.6 reduce-window.6
  8.1 0.2 slice_reduce_fusion
  8.4 0.1 fusion.24
  8.5 0.0 copy-done
  8.5 1.3 convolution_convert_fusion
  9.7 0.0 copy-start.3
  9.7 77.1 %all_to_all.10 = bf16[16,24,4096]{2,1,0:T(8,128)(2,1)S(1)} all-to-all(bf16[16,24,4096]{2,1,0:T(8,128)(2,1)S(1)} %bitcast.50), channel_id=1, replica_groups=mesh['dp'=2,'expert'=16] {'expert'}, dimensions={0} | all-to-all | bytes 6291456 | tf_op jit(solution)/shard_map/all_to_all | solution.py:28
  86.8 0.0 copy-start.1
  86.8 1.7 copy-done.1
  88.5 0.0 copy-done.3
  88.5 2.6 %fusion.4 = f32[384,768]{1,0:T(8,128)S(1)} fusion(bf16[384,4096]{1,0:T(8,128)(2,1)S(1)} %bitcast.52, bf16[1,4096,768]{2,1,0:T(8,128)(2,1)S(1)} %copy-done.3), kind=kOutput, calls=%fused_computation.5 | convolution fusion | flops 2415919104 | bytes 10616832 | tf_op jit(solution)/shard_map/dot_general | solution.py:36
  91.1 13.9 %fusion.6 = bf16[384,4096]{1,0:T(8,128)(2,1)} fusion(bf16[1,768,4096]{2,1,0:T(8,128)(2,1)} %param.11, bf16[384,4096]{1,0:T(8,128)(2,1)} %bitcast.53, bf16[1,4096,768]{2,1,0:T(8,128)(2,1)} %param.10, f32[384,768]{1,0:T(8,128)S(1)} %fusion.4), kind=kOutput, calls=%fused_computation.8 | convolution fusion | flops 4835180544 | bytes 20054016 | tf_op jit(solution)/shard_map/dot_general | solution.py:39
  105.0 0.0 copy-start.2
  105.0 5.4 %all-to-all-start.1 = ((bf16[16,24,4096]{2,1,0:T(8,128)(2,1)}), bf16[16,24,4096]{2,1,0:T(8,128)(2,1)S(1)}, u32[]{:S(2)}, u32[]{:S(2)}) async-start(bf16[16,24,4096]{2,1,0:T(8,128)(2,1)} %bitcast.51), calls=%async_computation.1 | async-start | bytes 6291456 | tf_op jit(solution)/shard_map/all_to_all | solution.py:42
  110.4 0.2 all-reduce.2.cloned.1.call-start
  110.6 0.1 reduce_sum.23
  110.7 0.1 mul.53
  110.8 0.0 copy-done.2
  110.8 0.1 copy.9
  110.9 58.7 %all-to-all-done.1 = bf16[16,24,4096]{2,1,0:T(8,128)(2,1)S(1)} async-done(((bf16[16,24,4096]{2,1,0:T(8,128)(2,1)}), bf16[16,24,4096]{2,1,0:T(8,128)(2,1)S(1)}, u32[]{:S(2)}, u32[]{:S(2)}) %all-to-all-start.1) | async-done | bytes 3145760 | tf_op jit(solution)/shard_map/all_to_all | solution.py:42
  169.6 3.2 %gather_fusion = bf16[256,4096]{1,0:T(8,128)(2,1)} fusion(bf16[384,4096]{1,0:T(8,128)(2,1)S(1)} %bitcast.49, s32[1024]{0:T(1024)S(1)} %pad_clamp_fusion), kind=kCustom, calls=%fused_computation | custom fusion | bytes 4195328 | tf_op jit(solution)/shard_map/jit(_take)/gather | solution.py:52
  172.8 4.2 %multiply_reduce_fusion = bf16[32,4096]{1,0:T(8,128)(2,1)} fusion(bf16[256,4096]{1,0:T(8,128)(2,1)} %gather_fusion, f32[32,8]{1,0:T(8,128)S(1)} %copy.9, pred[32,8]{1,0:T(8,128)(4,1)S(1)} %compare_and_fusion), kind=kLoop, calls=%fused_computation.9 | loop fusion | flops 4063232 | bytes 2360576 | tf_op jit(solution)/shard_map/reduce_sum | solution.py:56
  177.0 0.0 all-reduce.2.cloned.1.call-update
  177.0 34.2 %all-reduce.2.cloned.1.call-done = bf16[32,4096]{1,0:T(8,128)(2,1)} async-done(((bf16[32,4096]{1,0:T(8,128)(2,1)}), bf16[32,4096]{1,0:T(8,128)(2,1)}) %all-reduce.2.cloned.1.call-update) | async-done | bytes 262160 | tf_op jit(solution)/shard_map/psum | solution.py:57
  211.3 1.7 copy.17
  (9 shorter events, 0.1 us)
Async XLA Ops:
  6.5 1.9 copy-start
  9.7 78.8 %copy-start.3 = (bf16[1,4096,768]{2,1,0:T(8,128)(2,1)S(1)}, bf16[1,4096,768]{2,1,0:T(8,128)(2,1)}, u32[]{:S(2)}) copy-start(bf16[1,4096,768]{2,1,0:T(8,128)(2,1)} %param.9) | copy-start | bytes 18874372
  86.8 1.7 copy-start.1
  105.0 5.8 %copy-start.2 = (s32[32,8]{0,1:T(8,128)S(1)}, s32[32,8]{0,1:T(8,128)}, u32[]{:S(2)}) copy-start(s32[32,8]{0,1:T(8,128)} %param.8) | copy-start | bytes 3076
  105.0 64.6 %all-to-all-start.1 = ((bf16[16,24,4096]{2,1,0:T(8,128)(2,1)}), bf16[16,24,4096]{2,1,0:T(8,128)(2,1)S(1)}, u32[]{:S(2)}, u32[]{:S(2)}) async-start(bf16[16,24,4096]{2,1,0:T(8,128)(2,1)} %bitcast.51), calls=%async_computation.1 | async-start | bytes 6291456 | tf_op jit(solution)/shard_map/all_to_all | solution.py:42
  110.4 100.9 %all-reduce.2.cloned.1.call-start = ((), (), s32[]{:S(2)}) async-start(), calls=%async_computation.2 | async-start | bytes 524288 | tf_op jit(solution)/shard_map/psum | solution.py:57
Sparse Core Ops, SparseCore 0:
  177.2 34.0 all-reduce.1
where the time goes:
time: 220 us
  waiting for transfers between devices  92.9 us (42%)
  blocking collectives  77.1 us (35%)
  matrix products  17.7 us (8%)
  between operations  13.5 us (6%)
  local copies, waits for them, and re-layouts  7.96 us (4%)
  starting transfers between devices  5.58 us (3%)
  other arithmetic  4.97 us (2%)
    all_to_all x1, blocking collectives, on_device(): lax.all_to_all(outgoing.reshape(groups, capacity, feature), 'expert', spl...  77.1 us
    all_to_all x1, waiting for transfers between devices, on_device(): lax.all_to_all(partial_value.reshape(groups, capacity, feature), 'expert'...  58.7 us
    psum x1, waiting for transfers between devices, on_device(): mixed = lax.psum(local_mix.astype(jnp.bfloat16), 'dp')  34.2 us
    dot_general x1, matrix products, on_device(): jnp.dot(hidden, w_down[0], preferred_element_type=jnp.float32)  13.9 us
    all_to_all x1, starting transfers between devices, on_device(): lax.all_to_all(partial_value.reshape(groups, capacity, feature), 'expert'...  5.35 us
  transfers between devices with their start and end apart: 2, of which 2 were waited for; matrix products, arithmetic and copies ran while one was open for 0% of the time, Pallas kernels for 0%

commit v1 on v0

--- a/solution.py
+++ b/solution.py
@@ -4,7 +4,7 @@
 from jax.sharding import PartitionSpec as P
 
 
-def on_device(tokens, expert_ids, gate_ints, w_gate, w_up, w_down):
+def dispatch_form(tokens, expert_ids, gate_ints, w_gate, w_up, w_down):
     tok_rows = tokens.shape[0]
     top_count = expert_ids.shape[1]
     feature = tokens.shape[1]
@@ -58,6 +58,30 @@
     return mixed
 
 
+def dense_form(tokens, expert_ids, gate_ints, w_gate, w_up, w_down):
+    groups = lax.axis_size("expert")
+    me = lax.axis_index("expert")
+    chosen = expert_ids[:, :, None] == jnp.arange(groups, dtype=jnp.int32)[None, None, :]
+    coef = jnp.sum(jnp.where(chosen, gate_ints[:, :, None], 0), axis=1).astype(jnp.float32) / 1024.0
+    rows = lax.all_gather(tokens, "expert", axis=0, tiled=True)
+    coefs = lax.all_gather(coef, "expert", axis=0, tiled=True)
+    mine = lax.dynamic_slice_in_dim(coefs, me, 1, axis=1)
+    gate = jnp.dot(rows, w_gate[0], preferred_element_type=jnp.float32)
+    up = jnp.dot(rows, w_up[0], preferred_element_type=jnp.float32)
+    hidden = (jax.nn.silu(gate) * up).astype(jnp.bfloat16)
+    part = mine * jnp.dot(hidden, w_down[0], preferred_element_type=jnp.float32)
+    local = lax.psum_scatter(part.astype(jnp.bfloat16), "expert", scatter_dimension=0, tiled=True)
+    return lax.psum(local, "dp")
+
+
+def on_device(tokens, expert_ids, *rest):
+    tok_rows, top_count = expert_ids.shape
+    groups = lax.axis_size("expert")
+    capacity = min(tok_rows, max(2, 3 * tok_rows * top_count // (2 * groups)))
+    form = dense_form if tok_rows <= 2 * capacity else dispatch_form
+    return form(tokens, expert_ids, *rest)
+
+
 def solution(mesh):
     return jax.shard_map(
         on_device,

time: 220 us -> 191 us (0.87)
  blocking collectives: 77.1 us -> 23.6 us
  waiting for transfers between devices: 92.9 us -> 128 us
  local copies, waits for them, and re-layouts: 7.96 us -> 1.83 us
  matrix products: 17.7 us -> 23.6 us
  starting transfers between devices: 5.58 us -> 0.08 us
  other arithmetic: 4.97 us -> 0.73 us
    all_to_all x1 -> x0, blocking collectives: 77.1 us -> none  [on_device(): lax.all_to_all(outgoing.reshape(groups, capacity, feature), 'expert', spl...]
    reduce_scatter x0 -> x1, waiting for transfers between devices: none -> 71.4 us  [dense_form(): lax.psum_scatter(part.astype(jnp.bfloat16), 'expert', scatter_dimension=0...]
    all_to_all x1 -> x0, waiting for transfers between devices: 58.7 us -> none  [on_device(): lax.all_to_all(partial_value.reshape(groups, capacity, feature), 'expert'...]
    all_gather x0 -> x1, waiting for transfers between devices: none -> 30.9 us  [dense_form(): rows = lax.all_gather(tokens, 'expert', axis=0, tiled=True)]
    all_gather x0 -> x1, blocking collectives: none -> 23.6 us  [dense_form(): coefs = lax.all_gather(coef, 'expert', axis=0, tiled=True)]
    psum x1, waiting for transfers between devices: 34.2 us -> 24.6 us  [dense_form(): return lax.psum(local, 'dp')]
    dot_general x3 -> x2, matrix products: 17.7 us -> 23.6 us  [the longest x1 16.6 us: dense_form(): part = mine * jnp.dot(hidden, w_down[0], preferred_element_type=jnp.float32)]
    all_to_all x1 -> x0, starting transfers between devices: 5.35 us -> none  [on_device(): lax.all_to_all(partial_value.reshape(groups, capacity, feature), 'expert'...]
  transfers between devices with their start and end apart: 2 -> 3, of which waited for: 2 -> 3; matrix products, arithmetic and copies ran while one was open for 0% -> 0% of each run, Pallas kernels for 0% -> 0%
where the time goes in v1:
time: 191 us
  waiting for transfers between devices  128 us (67%)
  blocking collectives  23.6 us (12%)
  matrix products  23.6 us (12%)
  between operations  13.1 us (7%)
    reduce_scatter x1, waiting for transfers between devices, dense_form(): lax.psum_scatter(part.astype(jnp.bfloat16), 'expert', scatter_dimension=0...  71.4 us
    all_gather x1, waiting for transfers between devices, dense_form(): rows = lax.all_gather(tokens, 'expert', axis=0, tiled=True)  30.9 us
    psum x1, waiting for transfers between devices, dense_form(): return lax.psum(local, 'dp')  24.6 us
    all_gather x1, blocking collectives, dense_form(): coefs = lax.all_gather(coef, 'expert', axis=0, tiled=True)  23.6 us
    dot_general x1, matrix products, dense_form(): part = mine * jnp.dot(hidden, w_down[0], preferred_element_type=jnp.float32)  16.6 us
    dot_general x1, matrix products, dense_form(): gate = jnp.dot(rows, w_gate[0], preferred_element_type=jnp.float32)  7.03 us
  transfers between devices with their start and end apart: 3, of which 3 were waited for; matrix products, arithmetic and copies ran while one was open for 0% of the time, Pallas kernels for 0%

profile of v1, /device:TPU:0, one launch (start us, length us, event | category | flops | bytes accessed | tf_op | source)
XLA Modules:
  0.0 190.7 jit_solution(241557817520303641)
XLA Ops:
  6.5 0.0 all-gather.3.cloned.1.call-start
  6.5 0.7 all-gather.3.cloned.1.call-update
  7.3 0.0 reduce-scatter.2.cloned.1.call-start
  7.3 0.7 select_reduce_fusion
  8.0 23.6 %all-gather = f32[16,32,16]{1,2,0:T(8,128)S(1)} all-gather(f32[1,32,16]{1,2,0:T(8,128)S(1)} %multiply_bitcast_fusion), channel_id=1, replica_groups=mesh['dp'=2,'expert'=16] {'expert'}, dimensions={0}, use_global_device_ids=true | all-gather | bytes 34816 | tf_op jit(solution)/shard_map/all_gather | solution.py:67
  31.7 0.1 reshape.3
  31.9 30.9 %all-gather.3.cloned.1.call-done = bf16[512,4096]{1,0:T(8,128)(2,1)} async-done(((bf16[32,4096]{1,0:T(8,128)(2,1)}), bf16[512,4096]{1,0:T(8,128)(2,1)}) %all-gather.3.cloned.1.call-update) | async-done | bytes 4194320 | tf_op jit(solution)/shard_map/all_gather | solution.py:66
  62.8 7.0 %fusion.3 = f32[512,768]{1,0:T(8,128)S(1)} fusion(bf16[512,4096]{1,0:T(8,128)(2,1)} %all-gather.3.cloned.1.call-done, bf16[1,4096,768]{2,1,0:T(8,128)(2,1)} %param.9), kind=kOutput, calls=%fused_computation.4 | convolution fusion | flops 3221225472 | bytes 12058624 | tf_op jit(solution)/shard_map/dot_general | solution.py:69
  69.8 16.6 %multiply_convert_fusion = bf16[512,4096]{1,0:T(8,128)(2,1)} fusion(bf16[1,768,4096]{2,1,0:T(8,128)(2,1)} %param.11, f32[512]{0:T(512)S(1)} %bitcast.20, f32[512,768]{1,0:T(8,128)S(1)} %fusion.3, bf16[512,4096]{1,0:T(8,128)(2,1)} %all-gather.3.cloned.1.call-done, bf16[1,4096,768]{2,1,0:T(8,128)(2,1)} %param.10), kind=kOutput, calls=%fused_computation | convolution fusion | flops 6449004544 | bytes 22546432 | tf_op jit(solution)/shard_map/dot_general | solution.py:72
  86.4 0.0 reduce-scatter.2.cloned.1.call-update
  86.4 0.0 all-reduce.2.cloned.1.call-start
  86.5 71.4 %reduce-scatter.2.cloned.1.call-done = bf16[32,4096]{1,0:T(8,128)(2,1)} async-done(((bf16[512,4096]{1,0:T(8,128)(2,1)}), bf16[32,4096]{1,0:T(8,128)(2,1)}) %reduce-scatter.2.cloned.1.call-update) | async-done | bytes 262160 | tf_op jit(solution)/shard_map/reduce_scatter | solution.py:73
  157.9 0.0 all-reduce.2.cloned.1.call-update
  157.9 24.6 %all-reduce.2.cloned.1.call-done = bf16[32,4096]{1,0:T(8,128)(2,1)} async-done(((bf16[32,4096]{1,0:T(8,128)(2,1)}), bf16[32,4096]{1,0:T(8,128)(2,1)}) %all-reduce.2.cloned.1.call-update) | async-done | bytes 262160 | tf_op jit(solution)/shard_map/psum | solution.py:74
  182.5 1.7 copy.18
  (3 shorter events, 0.1 us)
Async XLA Ops:
  6.5 56.3 %all-gather.3.cloned.1.call-start = ((), (), s32[]{:S(2)}) async-start(), calls=%async_computation.1 | async-start | bytes 4456448 | tf_op jit(solution)/shard_map/all_gather | solution.py:66
  7.3 150.6 %reduce-scatter.2.cloned.1.call-start = ((), (), s32[]{:S(2)}) async-start(), calls=%async_computation.2 | async-start | bytes 4456448 | tf_op jit(solution)/shard_map/reduce_scatter | solution.py:73
  86.4 96.1 %all-reduce.2.cloned.1.call-start = ((), (), s32[]{:S(2)}) async-start(), calls=%async_computation.3 | async-start | bytes 524288 | tf_op jit(solution)/shard_map/psum | solution.py:74
Sparse Core Ops, SparseCore 0:
  9.5 53.2 all-gather.2
  86.6 71.2 reduce-scatter.1
  160.2 22.2 all-reduce.1

commit v2 on v0

--- a/solution.py
+++ b/solution.py
@@ -1,10 +1,322 @@
+import functools
+
 import jax
 import jax.numpy as jnp
 from jax import lax
+from jax.experimental import pallas as pl
+from jax.experimental.pallas import tpu as pltpu
 from jax.sharding import PartitionSpec as P
 
-
-def on_device(tokens, expert_ids, gate_ints, w_gate, w_up, w_down):
+LANES = 128
+CHUNKS = 4
+WEIGHT_PIECES = 4
+
+
+def ring_kernel(
+    groups, x_ref, wg_any, wu_any, wd_any, o_ref,
+    xall, wg, wu, wd, hid, part, quad, outgo, income, fin, other,
+    w_sem, own_sem, ag_send, ag_recv, core_send, core_recv,
+    quad_send, quad_recv, rs_send, rs_recv, dp_send, dp_recv,
+):
+    chips = groups // 2
+    half = chips // 2
+    block = x_ref.shape[0]
+    width = x_ref.shape[1]
+    feature = wg.shape[0]
+    hidden = wg.shape[1]
+    split = feature // 2
+    side = chips * block
+
+    me = lax.axis_index("expert")
+    plane = lax.axis_index("dp")
+    core = lax.rem(me, 2)
+    chip = lax.div(me, 2)
+    row, column = lax.rem(chip, 2), lax.div(chip, 2)
+    place = (1 - row) * column + row * (chips - 1 - column)
+
+    def expert_at(position):
+        back = lax.div(position, half)
+        there = (1 - back) * (2 * position) + back * (2 * (chips - 1 - position) + 1)
+        return there * 2 + core
+
+    right = {"expert": expert_at(lax.rem(place + 1, chips))}
+    left = {"expert": expert_at(lax.rem(place + chips - 1, chips))}
+    mate = {"expert": chip * 2 + (1 - core)}
+    twin = {"dp": 1 - plane}
+    sides = (right, left)
+
+    def send(src, dst, send_sem, recv_sem, device):
+        return pltpu.make_async_remote_copy(
+            src_ref=src, dst_ref=dst, send_sem=send_sem, recv_sem=recv_sem,
+            device_id=device, device_id_type=pl.DeviceIdType.MESH,
+        )
+
+    def local(index, src, dst):
+        rows = src.shape[1] // WEIGHT_PIECES
+        return [
+            pltpu.make_async_copy(
+                src.at[0, pl.ds(i * rows, rows)], dst.at[pl.ds(i * rows, rows)],
+                w_sem.at[index * WEIGHT_PIECES + i],
+            )
+            for i in range(WEIGHT_PIECES)
+        ]
+
+    loads = [local(0, wg_any, wg), local(1, wu_any, wu), local(2, wd_any, wd)]
+    own = pltpu.make_async_copy(x_ref, xall.at[pl.ds(0, block)], own_sem)
+    own.start()
+    for pieces in loads[:2]:
+        for piece in pieces:
+            piece.start()
+
+    barrier = pltpu.get_barrier_semaphore()
+    for device in (right, left, mate, twin):
+        pl.semaphore_signal(barrier, inc=1, device_id=device, device_id_type=pl.DeviceIdType.MESH)
+    pl.semaphore_wait(barrier, 4)
+
+    def rows_of(slot, which):
+        return pl.ds((2 * slot + which) * block, block)
+
+    def hop(way, step):
+        slot = 2 * step - 1 + way if step < half else chips - 1
+        columns = pl.ds(0, width) if step < half else (pl.ds(0, split), pl.ds(split, width - split))[way]
+        source = x_ref if step == 1 else xall.at[rows_of(2 * (step - 1) - 1 + way, 0)]
+        return send(
+            source.at[:, columns], xall.at[rows_of(slot, 0), columns],
+            ag_send.at[way * half + step - 1], ag_recv.at[way * half + step - 1], sides[way],
+        )
+
+    def share(slot, way=0):
+        index = slot + way
+        columns = pl.ds(0, width)
+        if slot == chips - 1:
+            columns = (pl.ds(0, split), pl.ds(split, width - split))[way]
+        source = x_ref if slot == 0 else xall.at[rows_of(slot, 0)]
+        return send(
+            source.at[:, columns], xall.at[rows_of(slot, 1), columns],
+            core_send.at[index], core_recv.at[index], mate,
+        )
+
+    hops = [[hop(way, step) for step in range(1, half + 1)] for way in range(2)]
+    shares = [share(slot) for slot in range(chips)] + [share(chips - 1, 1)]
+
+    hops[0][0].start()
+    hops[1][0].start()
+    shares[0].start()
+
+    tile = 256 if hidden % 256 == 0 else LANES
+
+    def expert_rows(first, count):
+        rows = pl.ds(2 * first * block, 2 * count * block)
+        marks = xall[rows, pl.ds(feature, width - feature)].astype(jnp.float32)
+        lane = lax.broadcasted_iota(jnp.int32, marks.shape, 1)
+        mine = jnp.logical_or(lane == me, lane == me + groups)
+        coef = jnp.sum(jnp.where(mine, marks, 0.0), axis=1, keepdims=True)
+
+        def body(t, carry):
+            columns = pl.ds(pl.multiple_of(t * tile, tile), tile)
+            values = xall[rows, pl.ds(0, feature)]
+            gate = jnp.dot(values, wg[:, columns], preferred_element_type=jnp.float32)
+            up = jnp.dot(values, wu[:, columns], preferred_element_type=jnp.float32)
+            out = (gate / (1.0 + jnp.exp(-gate)) * up * coef).astype(jnp.bfloat16)
+            for slot in range(count):
+                for which in range(2):
+                    start = (2 * slot + which) * block
+                    hid[pl.ds(which * side + (first + slot) * block, block), columns] = out[
+                        start : start + block
+                    ]
+            return carry
+
+        lax.fori_loop(0, hidden // tile, body, 0)
+
+    own.wait()
+    for step in range(1, half + 1):
+        for way in range(2):
+            hops[way][step - 1].wait_recv()
+            if step < half:
+                hops[way][step].start()
+                shares[2 * step - 1 + way].start()
+            else:
+                shares[chips - 1 + way].start()
+        if step == 1:
+            for pieces in loads[:2]:
+                for piece in pieces:
+                    piece.wait()
+            for piece in loads[2]:
+                piece.start()
+            shares[0].wait_recv()
+            expert_rows(0, 1)
+        else:
+            shares[2 * step - 3].wait_recv()
+            shares[2 * step - 2].wait_recv()
+            expert_rows(2 * step - 3, 2)
+    shares[chips - 1].wait_recv()
+    shares[chips].wait_recv()
+    expert_rows(chips - 1, 1)
+    for piece in loads[2]:
+        piece.wait()
+
+    span = feature // CHUNKS
+    part_tile = 256 if span % 256 == 0 else LANES
+
+    def project(chunk, which):
+        def body(t, carry):
+            columns = pl.ds(pl.multiple_of(chunk * span + t * part_tile, part_tile), part_tile)
+            part[pl.ds(which * side, side), columns] = jnp.dot(
+                hid[pl.ds(which * side, side), :], wd[:, columns],
+                preferred_element_type=jnp.float32,
+            ).astype(jnp.bfloat16)
+            return carry
+
+        lax.fori_loop(0, span // part_tile, body, 0)
+
+    def area(chunk):
+        return pl.ds(chunk * span, span)
+
+    def trade(chunk):
+        return send(
+            part.at[pl.ds(side, side), area(chunk)], quad.at[:, area(chunk)],
+            quad_send.at[chunk], quad_recv.at[chunk], mate,
+        )
+
+    def sums(slot, columns):
+        rows = pl.ds(slot * block, block)
+        return part[rows, columns].astype(jnp.float32) + quad[rows, columns].astype(jnp.float32)
+
+    def lot(way, reach):
+        return pl.ds((way * half + reach - 1) * block, block)
+
+    def ship(chunk, way, reach):
+        columns = area(chunk)
+        if reach == half:
+            columns = pl.ds(chunk * span + way * (span // 2), span // 2)
+        index = (way * half + reach - 1) * CHUNKS + chunk
+        return send(
+            outgo.at[lot(way, reach), columns], income.at[lot(way, reach), columns],
+            rs_send.at[index], rs_recv.at[index], sides[way],
+        )
+
+    def swap(chunk):
+        return send(
+            fin.at[:, area(chunk)], other.at[:, area(chunk)],
+            dp_send.at[chunk], dp_recv.at[chunk], twin,
+        )
+
+    trades = [trade(chunk) for chunk in range(CHUNKS)]
+    swaps = [swap(chunk) for chunk in range(CHUNKS)]
+    ships = {
+        (chunk, way, reach): ship(chunk, way, reach)
+        for chunk in range(CHUNKS) for way in range(2) for reach in range(1, half + 1)
+    }
+
+    def stage(chunk, number):
+        begin = chunk * span
+        if number == 0:
+            project(chunk, 1)
+            trades[chunk].start()
+            project(chunk, 0)
+        elif number == 1:
+            trades[chunk].wait_recv()
+            for way in range(2):
+                columns = pl.ds(begin + way * (span // 2), span // 2)
+                outgo[lot(way, half), columns] = sums(chips - 1, columns).astype(jnp.bfloat16)
+                ships[chunk, way, half].start()
+        elif number <= half:
+            reach = half + 1 - number
+            for way in range(2):
+                ships[chunk, way, reach + 1].wait_recv()
+                slot = 2 * reach - way
+                for piece in range(2):
+                    columns = pl.ds(begin + piece * (span // 2), span // 2)
+                    total = sums(slot, columns)
+                    if reach + 1 < half or piece == way:
+                        total = total + income[lot(way, reach + 1), columns].astype(jnp.float32)
+                    outgo[lot(way, reach), columns] = total.astype(jnp.bfloat16)
+                ships[chunk, way, reach].start()
+        elif number == half + 1:
+            ships[chunk, 0, 1].wait_recv()
+            ships[chunk, 1, 1].wait_recv()
+            columns = area(chunk)
+            total = sums(0, columns)
+            total = total + income[lot(0, 1), columns].astype(jnp.float32)
+            total = total + income[lot(1, 1), columns].astype(jnp.float32)
+            fin[:, columns] = total.astype(jnp.bfloat16)
+            swaps[chunk].start()
+        else:
+            swaps[chunk].wait_recv()
+            columns = area(chunk)
+            o_ref[:, columns] = (
+                fin[:, columns].astype(jnp.float32) + other[:, columns].astype(jnp.float32)
+            ).astype(jnp.bfloat16)
+
+    stages = half + 3
+    for wave in range(CHUNKS + stages - 1):
+        if wave < CHUNKS:
+            stage(wave, 0)
+        for chunk in range(CHUNKS):
+            if 0 < wave - chunk < stages:
+                stage(chunk, wave - chunk)
+
+    for copy in hops[0] + hops[1] + shares + trades + swaps + list(ships.values()):
+        copy.wait_send()
+
+
+def ring_form(tokens, expert_ids, gate_ints, w_gate, w_up, w_down):
+    groups = lax.axis_size("expert")
+    chips, half = groups // 2, groups // 4
+    block, feature = tokens.shape
+    hidden = w_gate.shape[2]
+    marks = -(-2 * groups // LANES) * LANES
+    lane = jnp.arange(marks, dtype=jnp.int32)[None, None, :]
+    high = gate_ints // 8 * 8
+    low = gate_ints - high
+    ids = expert_ids[:, :, None]
+    coef = jnp.sum(
+        jnp.where(ids == lane, high[:, :, None], 0)
+        + jnp.where(ids + groups == lane, low[:, :, None], 0),
+        axis=1,
+    )
+    coef = (coef.astype(jnp.float32) / 1024.0).astype(jnp.bfloat16)
+    x = jnp.concatenate([tokens, coef], axis=1)
+    width = feature + marks
+    rows = groups * block
+    dma = pltpu.SemaphoreType.DMA
+    return pl.pallas_call(
+        functools.partial(ring_kernel, groups),
+        out_shape=jax.ShapeDtypeStruct((block, feature), jnp.bfloat16),
+        in_specs=[pl.BlockSpec(memory_space=pltpu.VMEM)] + [pl.BlockSpec(memory_space=pl.ANY)] * 3,
+        out_specs=pl.BlockSpec(memory_space=pltpu.VMEM),
+        scratch_shapes=[
+            pltpu.VMEM((rows, width), jnp.bfloat16),
+            pltpu.VMEM((feature, hidden), jnp.bfloat16),
+            pltpu.VMEM((feature, hidden), jnp.bfloat16),
+            pltpu.VMEM((hidden, feature), jnp.bfloat16),
+            pltpu.VMEM((rows, hidden), jnp.bfloat16),
+            pltpu.VMEM((rows, feature), jnp.bfloat16),
+            pltpu.VMEM((chips * block, feature), jnp.bfloat16),
+            pltpu.VMEM((2 * half * block, feature), jnp.bfloat16),
+            pltpu.VMEM((2 * half * block, feature), jnp.bfloat16),
+            pltpu.VMEM((block, feature), jnp.bfloat16),
+            pltpu.VMEM((block, feature), jnp.bfloat16),
+            dma((3 * WEIGHT_PIECES,)),
+            dma,
+            dma((2 * half,)),
+            dma((2 * half,)),
+            dma((chips + 1,)),
+            dma((chips + 1,)),
+            dma((CHUNKS,)),
+            dma((CHUNKS,)),
+            dma((2 * half * CHUNKS,)),
+            dma((2 * half * CHUNKS,)),
+            dma((CHUNKS,)),
+            dma((CHUNKS,)),
+        ],
+        compiler_params=pltpu.CompilerParams(
+            collective_id=0, has_side_effects=True, vmem_limit_bytes=60 * 1024 * 1024
+        ),
+    )(x, w_gate, w_up, w_down)
+
+
+def dispatch_form(tokens, expert_ids, gate_ints, w_gate, w_up, w_down):
     tok_rows = tokens.shape[0]
     top_count = expert_ids.shape[1]
     feature = tokens.shape[1]
@@ -56,6 +368,15 @@
     local_mix = jnp.sum(weights * picked, axis=1)
     mixed = lax.psum(local_mix.astype(jnp.bfloat16), "dp")
     return mixed
+
+
+def on_device(tokens, expert_ids, *rest):
+    tok_rows, top_count = expert_ids.shape
+    groups = lax.axis_size("expert")
+    capacity = min(tok_rows, max(2, 3 * tok_rows * top_count // (2 * groups)))
+    fits = groups % 4 == 0 and groups >= 8 and lax.axis_size("dp") == 2
+    form = ring_form if fits and tok_rows <= 2 * capacity else dispatch_form
+    return form(tokens, expert_ids, *rest)
 
 
 def solution(mesh):

time: 220 us -> 81.7 us (0.37)
  waiting for transfers between devices: 92.9 us -> 0 us
  blocking collectives: 77.1 us -> 0 us
  Pallas kernels: 0 us -> 75.4 us
  matrix products: 17.7 us -> 0 us
  between operations: 13.5 us -> 0.02 us
  starting transfers between devices: 5.58 us -> 0 us
  local copies, waits for them, and re-layouts: 7.96 us -> 2.66 us
    all_to_all x1 -> x0, blocking collectives: 77.1 us -> none  [on_device(): lax.all_to_all(outgoing.reshape(groups, capacity, feature), 'expert', spl...]
    pallas_call x0 -> x1, Pallas kernels: none -> 75.4 us  [ring_form(): pl.pallas_call(functools.partial(ring_kernel, groups), out_shape=jax.Shap...]
    all_to_all x1 -> x0, waiting for transfers between devices: 58.7 us -> none  [on_device(): lax.all_to_all(partial_value.reshape(groups, capacity, feature), 'expert'...]
    psum x1 -> x0, waiting for transfers between devices: 34.2 us -> none  [on_device(): mixed = lax.psum(local_mix.astype(jnp.bfloat16), 'dp')]
    dot_general x3 -> x0, matrix products: 17.7 us -> none  [the longest x1 13.9 us: on_device(): jnp.dot(hidden, w_down[0], preferred_element_type=jnp.float32)]
    all_to_all x1 -> x0, starting transfers between devices: 5.35 us -> none  [on_device(): lax.all_to_all(partial_value.reshape(groups, capacity, feature), 'expert'...]
    reduce_sum x2 -> x1, other arithmetic: 4.29 us -> 0.21 us  [ring_form(): jnp.sum(jnp.where(ids == lane, high[:, :, None], 0) + jnp.where(ids + gro...]
    gather x1 -> x0, local copies, waits for them, and re-layouts: 3.2 us -> none  [on_device(): jnp.take(back_rows, target, axis=0).reshape(tok_rows, top_count, feature)]
  transfers between devices with their start and end apart: 2 -> 0, of which waited for: 2 -> 0; matrix products, arithmetic and copies ran while one was open for 0% -> 0% of each run, Pallas kernels for 0% -> 0%
where the time goes in v2:
time: 81.7 us; the launch traced here: 81.4 us
  Pallas kernels  75.4 us (92%)
  other arithmetic  3.27 us (4%)
  local copies, waits for them, and re-layouts  2.66 us (3%)
    pallas_call x1, Pallas kernels, ring_form(): pl.pallas_call(functools.partial(ring_kernel, groups), out_shape=jax.Shap...  75.4 us
    unnamed x2, local copies, waits for them, and re-layouts  2.43 us
    concatenate x1, other arithmetic, ring_form(): x = jnp.concatenate([tokens, coef], axis=1)  1.67 us

profile of v2, /device:TPU:0, one launch (start us, length us, event | category | flops | bytes accessed | tf_op | source)
XLA Modules:
  0.0 81.4 jit_solution(89378259566455224)
XLA Ops:
  0.0 0.7 broadcast_add_fusion
  0.7 0.7 fusion.1
  1.4 0.1 copy.12
  1.5 0.1 copy.13
  1.5 0.1 copy.14
  1.6 0.8 copy.11
  2.4 0.2 add_reduce_fusion
  2.6 1.7 %pad_maximum_fusion.x_ref = bf16[32,4224]{1,0:T(8,128)(2,1)} fusion(bf16[32,128]{1,0:T(8,128)(2,1)S(1)} %multiply_convert_fusion, bf16[32,4096]{1,0:T(8,128)(2,1)} %param.6), kind=kLoop, calls=%fused_computation | loop fusion | flops 540672 | bytes 540672 | tf_op jit(solution)/shard_map/concatenate | solution.py:279
  4.3 75.4 %shard_map.64 = bf16[32,4096]{1,0:T(8,128)(2,1)} custom-call(bf16[32,4224]{1,0:T(8,128)(2,1)} %pad_maximum_fusion.x_ref, bf16[1,4096,768]{2,1,0:T(8,128)(2,1)} %wg_any.1, bf16[1,4096,768]{2,1,0:T(8,128)(2,1)} %wu_any.1, bf16[1,768,4096]{2,1,0:T(8,128)(2,1)} %wd_any.1), custom_call_target="tpu_custom_call" | custom-call | tf_op jit(solution)/shard_map/pallas_call | solution.py:283
  79.7 1.7 %copy.16 = bf16[32,4096]{1,0:T(8,128)(2,1)} copy(bf16[32,4096]{1,0:T(8,128)(2,1)} %shard_map.64) | data formatting | bytes 524288
  (1 shorter events, 0.0 us)

commit v3 on v2

--- a/solution.py
+++ b/solution.py
@@ -9,22 +9,22 @@
 
 LANES = 128
 CHUNKS = 4
+PIECES = 2
 WEIGHT_PIECES = 4
 
 
 def ring_kernel(
-    groups, x_ref, wg_any, wu_any, wd_any, o_ref,
+    groups, x_any, ids_ref, gates_ref, wg_any, wu_any, wd_any, o_ref,
     xall, wg, wu, wd, hid, part, quad, outgo, income, fin, other,
     w_sem, own_sem, ag_send, ag_recv, core_send, core_recv,
     quad_send, quad_recv, rs_send, rs_recv, dp_send, dp_recv,
 ):
     chips = groups // 2
     half = chips // 2
-    block = x_ref.shape[0]
-    width = x_ref.shape[1]
+    block = x_any.shape[0]
+    width = xall.shape[1]
     feature = wg.shape[0]
     hidden = wg.shape[1]
-    split = feature // 2
     side = chips * block
 
     me = lax.axis_index("expert")
@@ -62,12 +62,25 @@
         ]
 
     loads = [local(0, wg_any, wg), local(1, wu_any, wu), local(2, wd_any, wd)]
-    own = pltpu.make_async_copy(x_ref, xall.at[pl.ds(0, block)], own_sem)
+    own = pltpu.make_async_copy(x_any, xall.at[pl.ds(0, block), pl.ds(0, feature)], own_sem)
     own.start()
     for pieces in loads[:2]:
         for piece in pieces:
             piece.start()
 
+    ids, gates = ids_ref[...], gates_ref[...]
+    low = jnp.bitwise_and(gates, 7)
+    high = gates - low
+    lane = lax.broadcasted_iota(jnp.int32, (block, width - feature), 1)
+    marks = jnp.zeros((block, width - feature), jnp.int32)
+    for k in range(ids.shape[1]):
+        chosen = ids[:, k : k + 1]
+        marks = marks + jnp.where(lane == chosen, high[:, k : k + 1], 0)
+        marks = marks + jnp.where(lane == chosen + groups, low[:, k : k + 1], 0)
+    xall[pl.ds(0, block), pl.ds(feature, width - feature)] = (
+        marks.astype(jnp.float32) / 1024.0
+    ).astype(jnp.bfloat16)
+
     barrier = pltpu.get_barrier_semaphore()
     for device in (right, left, mate, twin):
         pl.semaphore_signal(barrier, inc=1, device_id=device, device_id_type=pl.DeviceIdType.MESH)
@@ -76,32 +89,51 @@
     def rows_of(slot, which):
         return pl.ds((2 * slot + which) * block, block)
 
-    def hop(way, step):
-        slot = 2 * step - 1 + way if step < half else chips - 1
-        columns = pl.ds(0, width) if step < half else (pl.ds(0, split), pl.ds(split, width - split))[way]
-        source = x_ref if step == 1 else xall.at[rows_of(2 * (step - 1) - 1 + way, 0)]
+    def columns_of(piece):
+        begin = piece * (feature // PIECES)
+        end = width if piece == PIECES - 1 else begin + feature // PIECES
+        return pl.ds(begin, end - begin)
+
+    def carries(way, step, piece):
+        return step < half or piece // (PIECES // 2) == way
+
+    def slot_of(way, step):
+        return 0 if step == 0 else 2 * step - 1 + way if step < half else chips - 1
+
+    def hop(way, step, piece):
+        columns = columns_of(piece)
+        index = (way * half + step - 1) * PIECES + piece
         return send(
-            source.at[:, columns], xall.at[rows_of(slot, 0), columns],
-            ag_send.at[way * half + step - 1], ag_recv.at[way * half + step - 1], sides[way],
-        )
-
-    def share(slot, way=0):
-        index = slot + way
-        columns = pl.ds(0, width)
-        if slot == chips - 1:
-            columns = (pl.ds(0, split), pl.ds(split, width - split))[way]
-        source = x_ref if slot == 0 else xall.at[rows_of(slot, 0)]
+            xall.at[rows_of(slot_of(way, step - 1), 0), columns],
+            xall.at[rows_of(slot_of(way, step), 0), columns],
+            ag_send.at[index], ag_recv.at[index], sides[way],
+        )
+
+    def share(slot, piece):
+        columns = columns_of(piece)
+        index = slot * PIECES + piece
         return send(
-            source.at[:, columns], xall.at[rows_of(slot, 1), columns],
+            xall.at[rows_of(slot, 0), columns], xall.at[rows_of(slot, 1), columns],
             core_send.at[index], core_recv.at[index], mate,
         )
 
-    hops = [[hop(way, step) for step in range(1, half + 1)] for way in range(2)]
-    shares = [share(slot) for slot in range(chips)] + [share(chips - 1, 1)]
-
-    hops[0][0].start()
-    hops[1][0].start()
-    shares[0].start()
+    hops = {
+        (way, step, piece): hop(way, step, piece)
+        for step in range(1, half + 1) for piece in range(PIECES) for way in range(2)
+        if carries(way, step, piece)
+    }
+    shares = {(slot, piece): share(slot, piece) for slot in range(chips) for piece in range(PIECES)}
+
+    own.wait()
+    for piece in range(PIECES):
+        for way in range(2):
+            hops[way, 1, piece].start()
+    for piece in range(PIECES):
+        shares[0, piece].start()
+
+    def shared(slot):
+        for piece in range(PIECES):
+            shares[slot, piece].wait_recv()
 
     tile = 256 if hidden % 256 == 0 else LANES
 
@@ -128,29 +160,27 @@
 
         lax.fori_loop(0, hidden // tile, body, 0)
 
-    own.wait()
     for step in range(1, half + 1):
-        for way in range(2):
-            hops[way][step - 1].wait_recv()
-            if step < half:
-                hops[way][step].start()
-                shares[2 * step - 1 + way].start()
-            else:
-                shares[chips - 1 + way].start()
+        for piece in range(PIECES):
+            for way in range(2):
+                if (way, step, piece) in hops:
+                    hops[way, step, piece].wait_recv()
+                    if (way, step + 1, piece) in hops:
+                        hops[way, step + 1, piece].start()
+                    shares[slot_of(way, step), piece].start()
         if step == 1:
             for pieces in loads[:2]:
                 for piece in pieces:
                     piece.wait()
             for piece in loads[2]:
                 piece.start()
-            shares[0].wait_recv()
+            shared(0)
             expert_rows(0, 1)
         else:
-            shares[2 * step - 3].wait_recv()
-            shares[2 * step - 2].wait_recv()
+            shared(2 * step - 3)
+            shared(2 * step - 2)
             expert_rows(2 * step - 3, 2)
-    shares[chips - 1].wait_recv()
-    shares[chips].wait_recv()
+    shared(chips - 1)
     expert_rows(chips - 1, 1)
     for piece in loads[2]:
         piece.wait()
@@ -256,7 +286,7 @@
             if 0 < wave - chunk < stages:
                 stage(chunk, wave - chunk)
 
-    for copy in hops[0] + hops[1] + shares + trades + swaps + list(ships.values()):
+    for copy in list(hops.values()) + list(shares.values()) + trades + swaps + list(ships.values()):
         copy.wait_send()
 
 
@@ -266,24 +296,18 @@
     block, feature = tokens.shape
     hidden = w_gate.shape[2]
     marks = -(-2 * groups // LANES) * LANES
-    lane = jnp.arange(marks, dtype=jnp.int32)[None, None, :]
-    high = gate_ints // 8 * 8
-    low = gate_ints - high
-    ids = expert_ids[:, :, None]
-    coef = jnp.sum(
-        jnp.where(ids == lane, high[:, :, None], 0)
-        + jnp.where(ids + groups == lane, low[:, :, None], 0),
-        axis=1,
-    )
-    coef = (coef.astype(jnp.float32) / 1024.0).astype(jnp.bfloat16)
-    x = jnp.concatenate([tokens, coef], axis=1)
     width = feature + marks
     rows = groups * block
     dma = pltpu.SemaphoreType.DMA
     return pl.pallas_call(
         functools.partial(ring_kernel, groups),
         out_shape=jax.ShapeDtypeStruct((block, feature), jnp.bfloat16),
-        in_specs=[pl.BlockSpec(memory_space=pltpu.VMEM)] + [pl.BlockSpec(memory_space=pl.ANY)] * 3,
+        in_specs=[
+            pl.BlockSpec(memory_space=pl.ANY),
+            pl.BlockSpec(memory_space=pltpu.VMEM),
+            pl.BlockSpec(memory_space=pltpu.VMEM),
+        ]
+        + [pl.BlockSpec(memory_space=pl.ANY)] * 3,
         out_specs=pl.BlockSpec(memory_space=pltpu.VMEM),
         scratch_shapes=[
             pltpu.VMEM((rows, width), jnp.bfloat16),
@@ -299,10 +323,10 @@
             pltpu.VMEM((block, feature), jnp.bfloat16),
             dma((3 * WEIGHT_PIECES,)),
             dma,
-            dma((2 * half,)),
-            dma((2 * half,)),
-            dma((chips + 1,)),
-            dma((chips + 1,)),
+            dma((2 * half * PIECES,)),
+            dma((2 * half * PIECES,)),
+            dma((chips * PIECES,)),
+            dma((chips * PIECES,)),
             dma((CHUNKS,)),
             dma((CHUNKS,)),
             dma((2 * half * CHUNKS,)),
@@ -313,7 +337,7 @@
         compiler_params=pltpu.CompilerParams(
             collective_id=0, has_side_effects=True, vmem_limit_bytes=60 * 1024 * 1024
         ),
-    )(x, w_gate, w_up, w_down)
+    )(tokens, expert_ids, gate_ints, w_gate, w_up, w_down)
 
 
 def dispatch_form(tokens, expert_ids, gate_ints, w_gate, w_up, w_down):

time: 81.7 us -> 78.2 us (0.957)
  other arithmetic: 3.27 us -> 0 us
  Pallas kernels: 75.4 us -> 73.4 us
  local copies, waits for them, and re-layouts: 2.66 us -> 4.39 us
    pallas_call x1, Pallas kernels: 75.4 us -> 73.4 us  [ring_form(): pl.pallas_call(functools.partial(ring_kernel, groups), out_shape=jax.Shap...]
    unnamed x2 -> x3, local copies, waits for them, and re-layouts: 2.43 us -> 4.39 us
    concatenate x1 -> x0, other arithmetic: 1.67 us -> none  [ring_form(): x = jnp.concatenate([tokens, coef], axis=1)]
where the time goes in v3:
time: 78.2 us; the launch traced here: 77.8 us
  Pallas kernels  73.4 us (94%)
  local copies, waits for them, and re-layouts  4.39 us (6%)
    pallas_call x1, Pallas kernels, ring_form(): pl.pallas_call(functools.partial(ring_kernel, groups), out_shape=jax.Shap...  73.4 us
    unnamed x3, local copies, waits for them, and re-layouts  4.39 us

profile of v3, /device:TPU:0, one launch (start us, length us, event | category | flops | bytes accessed | tf_op | source)
XLA Modules:
  0.0 77.8 jit_solution(12947700913048626961)
XLA Ops:
  0.0 1.4 %copy.7.ids_ref = s32[32,8]{1,0:T(8,128)} copy(s32[32,8]{0,1:T(8,128)} %param.7) | data formatting | bytes 2048 | tf_op args[1]
  1.4 1.4 %copy.8.gates_ref = s32[32,8]{1,0:T(8,128)} copy(s32[32,8]{0,1:T(8,128)} %param.8) | data formatting | bytes 2048 | tf_op args[2]
  2.7 73.4 %shard_map.64 = bf16[32,4096]{1,0:T(8,128)(2,1)} custom-call(bf16[32,4096]{1,0:T(8,128)(2,1)} %x_any.1, s32[32,8]{1,0:T(8,128)} %copy.7.ids_ref, s32[32,8]{1,0:T(8,128)} %copy.8.gates_ref, bf16[1,4096,768]{2,1,0:T(8,128)(2,1)} %wg_any.1, bf16[1,4096,768]{2,1,0:T(8,128)(2,1)} %wu_any.1, bf16[1,768,4096]{2,1,0:T(8,128)(2,1)} %wd_any.1), custom_call_target="tpu_custom_call" | custom-call | tf_op jit(solution)/shard_map/pallas_call | solution.py:302
  76.2 1.7 %copy.10 = bf16[32,4096]{1,0:T(8,128)(2,1)} copy(bf16[32,4096]{1,0:T(8,128)(2,1)} %shard_map.64) | data formatting | bytes 524288

commit v4 on v3

--- a/solution.py
+++ b/solution.py
@@ -15,9 +15,9 @@
 
 def ring_kernel(
     groups, x_any, ids_ref, gates_ref, wg_any, wu_any, wd_any, o_ref,
-    xall, wg, wu, wd, hid, part, quad, outgo, income, fin, other,
+    xall, wg, wu, wd, hid, part, quad, outgo, income, fin, other, gift, gained,
     w_sem, own_sem, ag_send, ag_recv, core_send, core_recv,
-    quad_send, quad_recv, rs_send, rs_recv, dp_send, dp_recv,
+    quad_send, quad_recv, rs_send, rs_recv, dp_send, dp_recv, gift_send, gift_recv,
 ):
     chips = groups // 2
     half = chips // 2
@@ -188,9 +188,18 @@
     span = feature // CHUNKS
     part_tile = 256 if span % 256 == 0 else LANES
 
+    last = CHUNKS - 1
+    starts = [(1 - plane) * (last * span)] + [k * span for k in range(1, last)] + [plane * (last * span)]
+
+    def at(chunk, offset, count):
+        begin = starts[chunk] + offset
+        if chunk in (0, last):
+            begin = pl.multiple_of(begin, LANES)
+        return pl.ds(begin, count)
+
     def project(chunk, which):
         def body(t, carry):
-            columns = pl.ds(pl.multiple_of(chunk * span + t * part_tile, part_tile), part_tile)
+            columns = pl.ds(pl.multiple_of(starts[chunk] + t * part_tile, part_tile), part_tile)
             part[pl.ds(which * side, side), columns] = jnp.dot(
                 hid[pl.ds(which * side, side), :], wd[:, columns],
                 preferred_element_type=jnp.float32,
@@ -200,7 +209,7 @@
         lax.fori_loop(0, span // part_tile, body, 0)
 
     def area(chunk):
-        return pl.ds(chunk * span, span)
+        return at(chunk, 0, span)
 
     def trade(chunk):
         return send(
@@ -208,9 +217,18 @@
             quad_send.at[chunk], quad_recv.at[chunk], mate,
         )
 
-    def sums(slot, columns):
+    def sums(chunk, slot, offset, count):
+        rows, columns = pl.ds(slot * block, block), at(chunk, offset, count)
+        total = part[rows, columns].astype(jnp.float32) + quad[rows, columns].astype(jnp.float32)
+        if chunk == last:
+            total = total + gained[rows, pl.ds(offset, count)].astype(jnp.float32)
+        return total
+
+    def give(slot):
         rows = pl.ds(slot * block, block)
-        return part[rows, columns].astype(jnp.float32) + quad[rows, columns].astype(jnp.float32)
+        return send(
+            gift.at[rows], gained.at[rows], gift_send.at[slot], gift_recv.at[slot], twin
+        )
 
     def lot(way, reach):
         return pl.ds((way * half + reach - 1) * block, block)
@@ -218,7 +236,7 @@
     def ship(chunk, way, reach):
         columns = area(chunk)
         if reach == half:
-            columns = pl.ds(chunk * span + way * (span // 2), span // 2)
+            columns = at(chunk, way * (span // 2), span // 2)
         index = (way * half + reach - 1) * CHUNKS + chunk
         return send(
             outgo.at[lot(way, reach), columns], income.at[lot(way, reach), columns],
@@ -231,33 +249,45 @@
             dp_send.at[chunk], dp_recv.at[chunk], twin,
         )
 
+    gifts = [give(slot) for slot in range(chips)]
     trades = [trade(chunk) for chunk in range(CHUNKS)]
-    swaps = [swap(chunk) for chunk in range(CHUNKS)]
+    swaps = {chunk: swap(chunk) for chunk in range(1, CHUNKS)}
     ships = {
         (chunk, way, reach): ship(chunk, way, reach)
-        for chunk in range(CHUNKS) for way in range(2) for reach in range(1, half + 1)
+        for chunk in range(1, CHUNKS) for way in range(2) for reach in range(1, half + 1)
     }
 
     def stage(chunk, number):
-        begin = chunk * span
         if number == 0:
             project(chunk, 1)
             trades[chunk].start()
             project(chunk, 0)
+        elif number == 1 and chunk == 0:
+            trades[chunk].wait_recv()
+            for slot in reversed(range(chips)):
+                gift[pl.ds(slot * block, block), :] = sums(0, slot, 0, span).astype(jnp.bfloat16)
+                gifts[slot].start()
+        elif chunk == 0:
+            pass
         elif number == 1:
             trades[chunk].wait_recv()
+            if chunk == last:
+                gifts[chips - 1].wait_recv()
             for way in range(2):
-                columns = pl.ds(begin + way * (span // 2), span // 2)
-                outgo[lot(way, half), columns] = sums(chips - 1, columns).astype(jnp.bfloat16)
+                columns = at(chunk, way * (span // 2), span // 2)
+                total = sums(chunk, chips - 1, way * (span // 2), span // 2)
+                outgo[lot(way, half), columns] = total.astype(jnp.bfloat16)
                 ships[chunk, way, half].start()
         elif number <= half:
             reach = half + 1 - number
             for way in range(2):
                 ships[chunk, way, reach + 1].wait_recv()
                 slot = 2 * reach - way
+                if chunk == last:
+                    gifts[slot].wait_recv()
                 for piece in range(2):
-                    columns = pl.ds(begin + piece * (span // 2), span // 2)
-                    total = sums(slot, columns)
+                    columns = at(chunk, piece * (span // 2), span // 2)
+                    total = sums(chunk, slot, piece * (span // 2), span // 2)
                     if reach + 1 < half or piece == way:
                         total = total + income[lot(way, reach + 1), columns].astype(jnp.float32)
                     outgo[lot(way, reach), columns] = total.astype(jnp.bfloat16)
@@ -266,7 +296,9 @@
             ships[chunk, 0, 1].wait_recv()
             ships[chunk, 1, 1].wait_recv()
             columns = area(chunk)
-            total = sums(0, columns)
+            if chunk == last:
+                gifts[0].wait_recv()
+            total = sums(chunk, 0, 0, span)
             total = total + income[lot(0, 1), columns].astype(jnp.float32)
             total = total + income[lot(1, 1), columns].astype(jnp.float32)
             fin[:, columns] = total.astype(jnp.bfloat16)
@@ -274,6 +306,10 @@
         else:
             swaps[chunk].wait_recv()
             columns = area(chunk)
+            if chunk == last:
+                o_ref[:, columns] = fin[:, columns]
+                o_ref[:, area(0)] = other[:, area(0)]
+                return
             o_ref[:, columns] = (
                 fin[:, columns].astype(jnp.float32) + other[:, columns].astype(jnp.float32)
             ).astype(jnp.bfloat16)
@@ -286,7 +322,8 @@
             if 0 < wave - chunk < stages:
                 stage(chunk, wave - chunk)
 
-    for copy in list(hops.values()) + list(shares.values()) + trades + swaps + list(ships.values()):
+    copies = list(hops.values()) + list(shares.values()) + trades
+    for copy in copies + gifts + list(swaps.values()) + list(ships.values()):
         copy.wait_send()
 
 
@@ -321,6 +358,8 @@
             pltpu.VMEM((2 * half * block, feature), jnp.bfloat16),
             pltpu.VMEM((block, feature), jnp.bfloat16),
             pltpu.VMEM((block, feature), jnp.bfloat16),
+            pltpu.VMEM((chips * block, feature // CHUNKS), jnp.bfloat16),
+            pltpu.VMEM((chips * block, feature // CHUNKS), jnp.bfloat16),
             dma((3 * WEIGHT_PIECES,)),
             dma,
             dma((2 * half * PIECES,)),
@@ -333,6 +372,8 @@
             dma((2 * half * CHUNKS,)),
             dma((CHUNKS,)),
             dma((CHUNKS,)),
+            dma((chips,)),
+            dma((chips,)),
         ],
         compiler_params=pltpu.CompilerParams(
             collective_id=0, has_side_effects=True, vmem_limit_bytes=60 * 1024 * 1024

time: 78.2 us -> 75.8 us (0.969)
  Pallas kernels: 73.4 us -> 71 us
    pallas_call x1, Pallas kernels: 73.4 us -> 71 us  [ring_form(): pl.pallas_call(functools.partial(ring_kernel, groups), out_shape=jax.Shap...]
where the time goes in v4:
time: 75.8 us; the launch traced here: 75.4 us
  Pallas kernels  71 us (94%)
  local copies, waits for them, and re-layouts  4.39 us (6%)
    pallas_call x1, Pallas kernels, ring_form(): pl.pallas_call(functools.partial(ring_kernel, groups), out_shape=jax.Shap...  71 us
    unnamed x3, local copies, waits for them, and re-layouts  4.39 us

profile of v4, /device:TPU:0, one launch (start us, length us, event | category | flops | bytes accessed | tf_op | source)
XLA Modules:
  0.0 75.4 jit_solution(18006850676675913691)
XLA Ops:
  0.0 1.4 %copy.7.ids_ref = s32[32,8]{1,0:T(8,128)} copy(s32[32,8]{0,1:T(8,128)} %param.7) | data formatting | bytes 2048 | tf_op args[1]
  1.4 1.4 %copy.8.gates_ref = s32[32,8]{1,0:T(8,128)} copy(s32[32,8]{0,1:T(8,128)} %param.8) | data formatting | bytes 2048 | tf_op args[2]
  2.7 71.0 %shard_map.64 = bf16[32,4096]{1,0:T(8,128)(2,1)} custom-call(bf16[32,4096]{1,0:T(8,128)(2,1)} %x_any.1, s32[32,8]{1,0:T(8,128)} %copy.7.ids_ref, s32[32,8]{1,0:T(8,128)} %copy.8.gates_ref, bf16[1,4096,768]{2,1,0:T(8,128)(2,1)} %wg_any.1, bf16[1,4096,768]{2,1,0:T(8,128)(2,1)} %wu_any.1, bf16[1,768,4096]{2,1,0:T(8,128)(2,1)} %wd_any.1), custom_call_target="tpu_custom_call" | custom-call | tf_op jit(solution)/shard_map/pallas_call | solution.py:339
  73.7 1.7 %copy.10 = bf16[32,4096]{1,0:T(8,128)(2,1)} copy(bf16[32,4096]{1,0:T(8,128)(2,1)} %shard_map.64) | data formatting | bytes 524288

commit v5 on v4

--- a/solution.py
+++ b/solution.py
@@ -9,7 +9,7 @@
 
 LANES = 128
 CHUNKS = 4
-PIECES = 2
+PIECES = 4
 WEIGHT_PIECES = 4
 
 
@@ -17,7 +17,7 @@
     groups, x_any, ids_ref, gates_ref, wg_any, wu_any, wd_any, o_ref,
     xall, wg, wu, wd, hid, part, quad, outgo, income, fin, other, gift, gained,
     w_sem, own_sem, ag_send, ag_recv, core_send, core_recv,
-    quad_send, quad_recv, rs_send, rs_recv, dp_send, dp_recv, gift_send, gift_recv,
+    quad_send, quad_recv, rs_send, rs_recv, dp_send, dp_recv, gift_send, gift_recv, cross_send, cross_recv,
 ):
     chips = groups // 2
     half = chips // 2
@@ -90,12 +90,17 @@
         return pl.ds((2 * slot + which) * block, block)
 
     def columns_of(piece):
+        if piece < 2:
+            begin = (plane if piece == 0 else 1 - plane) * (feature // PIECES)
+            return pl.ds(pl.multiple_of(begin, LANES), feature // PIECES)
         begin = piece * (feature // PIECES)
         end = width if piece == PIECES - 1 else begin + feature // PIECES
         return pl.ds(begin, end - begin)
 
     def carries(way, step, piece):
-        return step < half or piece // (PIECES // 2) == way
+        if piece == 1:
+            return False
+        return step < half or (piece == PIECES - 1) == (way == 1)
 
     def slot_of(way, step):
         return 0 if step == 0 else 2 * step - 1 + way if step < half else chips - 1
@@ -124,10 +129,21 @@
     }
     shares = {(slot, piece): share(slot, piece) for slot in range(chips) for piece in range(PIECES)}
 
+    def cross(slot):
+        area = xall.at[rows_of(slot, 0), columns_of(0)]
+        return send(area, area, cross_send.at[slot], cross_recv.at[slot], twin)
+
+    crosses = {slot: cross(slot) for slot in range(1, chips)}
+
+    def crossed(slot):
+        crosses[slot].wait_recv()
+        shares[slot, 1].start()
+
     own.wait()
     for piece in range(PIECES):
         for way in range(2):
-            hops[way, 1, piece].start()
+            if (way, 1, piece) in hops:
+                hops[way, 1, piece].start()
     for piece in range(PIECES):
         shares[0, piece].start()
 
@@ -161,12 +177,17 @@
         lax.fori_loop(0, hidden // tile, body, 0)
 
     for step in range(1, half + 1):
+        if step > 1:
+            for way in range(2):
+                crossed(slot_of(way, step - 1))
         for piece in range(PIECES):
             for way in range(2):
                 if (way, step, piece) in hops:
                     hops[way, step, piece].wait_recv()
                     if (way, step + 1, piece) in hops:
                         hops[way, step + 1, piece].start()
+                    if piece == 0:
+                        crosses[slot_of(way, step)].start()
                     shares[slot_of(way, step), piece].start()
         if step == 1:
             for pieces in loads[:2]:
@@ -180,6 +201,7 @@
             shared(2 * step - 3)
             shared(2 * step - 2)
             expert_rows(2 * step - 3, 2)
+    crossed(chips - 1)
     shared(chips - 1)
     expert_rows(chips - 1, 1)
     for piece in loads[2]:
@@ -323,7 +345,7 @@
                 stage(chunk, wave - chunk)
 
     copies = list(hops.values()) + list(shares.values()) + trades
-    for copy in copies + gifts + list(swaps.values()) + list(ships.values()):
+    for copy in copies + list(crosses.values()) + gifts + list(swaps.values()) + list(ships.values()):
         copy.wait_send()
 
 
@@ -374,6 +396,8 @@
             dma((CHUNKS,)),
             dma((chips,)),
             dma((chips,)),
+            dma((chips,)),
+            dma((chips,)),
         ],
         compiler_params=pltpu.CompilerParams(
             collective_id=0, has_side_effects=True, vmem_limit_bytes=60 * 1024 * 1024

time: 75.8 us -> 72.8 us (0.960)
  Pallas kernels: 71 us -> 68 us
    pallas_call x1, Pallas kernels: 71 us -> 68 us  [ring_form(): pl.pallas_call(functools.partial(ring_kernel, groups), out_shape=jax.Shap...]
where the time goes in v5:
time: 72.8 us; the launch traced here: 72.4 us
  Pallas kernels  68 us (93%)
  local copies, waits for them, and re-layouts  4.39 us (6%)
    pallas_call x1, Pallas kernels, ring_form(): pl.pallas_call(functools.partial(ring_kernel, groups), out_shape=jax.Shap...  68 us
    unnamed x3, local copies, waits for them, and re-layouts  4.39 us

profile of v5, /device:TPU:0, one launch (start us, length us, event | category | flops | bytes accessed | tf_op | source)
XLA Modules:
  0.0 72.4 jit_solution(11169835958318598524)
XLA Ops:
  0.0 1.4 %copy.7.ids_ref = s32[32,8]{1,0:T(8,128)} copy(s32[32,8]{0,1:T(8,128)} %param.7) | data formatting | bytes 2048 | tf_op args[1]
  1.4 1.4 %copy.8.gates_ref = s32[32,8]{1,0:T(8,128)} copy(s32[32,8]{0,1:T(8,128)} %param.8) | data formatting | bytes 2048 | tf_op args[2]
  2.7 68.0 %shard_map.64 = bf16[32,4096]{1,0:T(8,128)(2,1)} custom-call(bf16[32,4096]{1,0:T(8,128)(2,1)} %x_any.1, s32[32,8]{1,0:T(8,128)} %copy.7.ids_ref, s32[32,8]{1,0:T(8,128)} %copy.8.gates_ref, bf16[1,4096,768]{2,1,0:T(8,128)(2,1)} %wg_any.1, bf16[1,4096,768]{2,1,0:T(8,128)(2,1)} %wu_any.1, bf16[1,768,4096]{2,1,0:T(8,128)(2,1)} %wd_any.1), custom_call_target="tpu_custom_call" | custom-call | tf_op jit(solution)/shard_map/pallas_call | solution.py:361
  70.8 1.7 %copy.10 = bf16[32,4096]{1,0:T(8,128)(2,1)} copy(bf16[32,4096]{1,0:T(8,128)(2,1)} %shard_map.64) | data formatting | bytes 524288
